TPU v7x, 256 devices: a whole 4x4x8 slice. The times are simulated.
256 devices in a mesh: group: 16 (over x, z_hi, core), blk: 16 (over y, z_lo).
Axes of the slice: x: 4, y: 4, z: 8 (z_hi: 2, z_lo: 4; z = z_hi * 4 + z_lo), core: 2. Of those that a mesh axis runs over, the one named last changes fastest.
Arguments:
- tokens: bfloat16 [12288, 7168], P(('group', 'blk')), may hold values from -6 to 6
- cotangent: bfloat16 [12288, 7168], P(('group', 'blk')), may hold values from -6 to 6
- w_gate: bfloat16 [16, 7168, 2048], P('group', None, 'blk'), may hold values from -0.0625 to 0.0625
- w_up: bfloat16 [16, 7168, 2048], P('group', None, 'blk'), may hold values from -0.0625 to 0.0625
- w_down: bfloat16 [16, 2048, 7168], P('group', 'blk'), may hold values from -0.125 to 0.125
- gate_weight: float32 [256, 16, 2], P(('group', 'blk')), may hold values from 0.1 to 1
- counts: int32 [256, 16], P(('group', 'blk')), may hold values from 0 to 2, as said below
- slots: int32 [256, 16, 2], P(('group', 'blk')), may hold values from 0 to 47, as said below
Outputs:
- grad_tokens: bfloat16 [12288, 7168], P(('group', 'blk'))
- grad_gate: bfloat16 [16, 7168, 2048], P('group', None, 'blk')
- grad_up: bfloat16 [16, 7168, 2048], P('group', None, 'blk')
- grad_down: bfloat16 [16, 2048, 7168], P('group', 'blk')
Inputs may be any that keep to these rules, and one draw needn't show every extreme that they name: `counts`: in every draw one expert has 2 tokens from every device. `slots`: the 2 entries of one device's list for one expert are different tokens.
All inputs are finite; a program needn't handle non-finite values.
Results may differ from a plain program's by a relative error of at most 0.018.
Values may be sent and summed in bfloat16 or wider, within the bound.
A program may use at most 128 MiB of HBM per device.

v0:
```python
import jax
import jax.numpy as jnp
from jax import lax
from jax.sharding import PartitionSpec as P


def contract_rows(left, right):
    return lax.dot_general(
        left, right, (((0,), (0,)), ((), ())), preferred_element_type=jnp.float32
    )


def contract_cols(left, right):
    return lax.dot_general(
        left, right, (((1,), (1,)), ((), ())), preferred_element_type=jnp.float32
    )


def body(tokens, cotangent, w_gate, w_up, w_down, gate_weight, counts, slots):
    experts = counts.shape[1]
    cap = slots.shape[2]
    tok_dev = tokens.shape[0]
    width = tokens.shape[1]
    position = lax.broadcasted_iota(jnp.int32, (experts, cap), 1)
    live = jnp.where(position < counts[0][:, None], gate_weight[0], jnp.zeros_like(gate_weight[0]))
    flat_slots = slots[0].reshape(experts * cap)
    rows_in = jnp.take(tokens, flat_slots, axis=0)
    scaled = (
        live.reshape(-1, 1) * jnp.take(cotangent, flat_slots, axis=0).astype(jnp.float32)
    ).astype(jnp.bfloat16)
    recv_in, recv_scaled = (
        lax.all_to_all(
            rows_in.reshape(experts, cap, width), "group", split_axis=0, concat_axis=0, tiled=True
        ),
        lax.all_to_all(
            scaled.reshape(experts, cap, width), "group", split_axis=0, concat_axis=0, tiled=True
        ),
    )
    groups = recv_in.shape[0]
    per_block = groups * cap
    gate_mat = w_gate[0]
    up_mat = w_up[0]
    down_mat = w_down[0]
    piece_in = lax.all_gather(recv_in[None], "blk", axis=0, tiled=True)
    piece_scaled = lax.all_gather(recv_scaled[None], "blk", axis=0, tiled=True)
    count = piece_in.shape[0]
    flat_in = piece_in.reshape(count * per_block, width)
    flat_scaled = piece_scaled.reshape(count * per_block, width)
    pre_gate = jnp.dot(flat_in, gate_mat, preferred_element_type=jnp.float32)
    pre_up = jnp.dot(flat_in, up_mat, preferred_element_type=jnp.float32)
    sigma = jax.nn.sigmoid(pre_gate)
    silu_val = pre_gate * sigma
    act = (silu_val * pre_up).astype(jnp.bfloat16)
    grad_hidden = contract_cols(flat_scaled, down_mat)
    grad_pre_gate = (grad_hidden * pre_up * sigma * (1.0 + pre_gate * (1.0 - sigma))).astype(
        jnp.bfloat16
    )
    grad_pre_up = (grad_hidden * silu_val).astype(jnp.bfloat16)
    acc_gate = contract_rows(flat_in, grad_pre_gate)
    acc_up = contract_rows(flat_in, grad_pre_up)
    acc_down = contract_rows(act, flat_scaled)
    block_part = contract_cols(grad_pre_gate, gate_mat) + contract_cols(grad_pre_up, up_mat)
    block_part = block_part.astype(jnp.bfloat16).reshape(count, per_block, width)
    partial_value = block_part
    acc_gate, acc_up, acc_down, partial_value = (acc_gate, acc_up, acc_down, partial_value)
    summed = lax.psum_scatter(
        partial_value.astype(jnp.float32).astype(jnp.bfloat16),
        "blk",
        scatter_dimension=0,
        tiled=True,
    ).astype(jnp.float32)
    slot_grad = lax.all_to_all(
        summed.reshape(groups, cap, width).astype(jnp.bfloat16),
        "group",
        split_axis=0,
        concat_axis=0,
        tiled=True,
    ).astype(jnp.float32)
    picker = (
        flat_slots[None, :] == lax.broadcasted_iota(jnp.int32, (tok_dev, experts * cap), 0)
    ).astype(jnp.float32)
    grad_tokens = jnp.dot(
        picker,
        slot_grad.reshape(experts * cap, width),
        precision=lax.Precision.HIGHEST,
        preferred_element_type=jnp.float32,
    )
    return (
        grad_tokens.astype(jnp.bfloat16),
        acc_gate.astype(jnp.bfloat16)[None],
        acc_up.astype(jnp.bfloat16)[None],
        acc_down.astype(jnp.bfloat16)[None],
    )


def solution(mesh):
    in_specs = (
        P(("group", "blk"), None),
        P(("group", "blk"), None),
        P("group", None, "blk"),
        P("group", None, "blk"),
        P("group", "blk", None),
        P(("group", "blk"), None, None),
        P(("group", "blk"), None),
        P(("group", "blk"), None, None),
    )
    out_specs = (
        P(("group", "blk"), None),
        P("group", None, "blk"),
        P("group", None, "blk"),
        P("group", "blk", None),
    )
    return jax.shard_map(body, mesh=mesh, in_specs=in_specs, out_specs=out_specs, check_vma=False)
```

profile of v0, /device:TPU:1, one launch (start us, length us, event | category | flops | bytes accessed | tf_op | source)
XLA Modules:
  0.0 607.4 jit_solution(10894749747023758770)
XLA Ops:
  7.3 0.9 copy.16
  8.2 0.1 eq.10
  8.3 2.4 gather_fusion.1
  10.7 0.1 broadcast_select_fusion
  10.9 0.2 reshape.57
  11.0 26.5 %all_to_all.15 = bf16[16,2,7168]{2,1,0:T(2,128)(2,1)} all-to-all(bf16[16,2,7168]{2,1,0:T(2,128)(2,1)S(1)} %reshape.57), channel_id=1, replica_groups=mesh['group'=16,'blk'=16] {'group'}, dimensions={0} | all-to-all | bytes 917504 | tf_op jit(solution)/shard_map/all_to_all | solution.py:32
  37.7 0.1 lt.26
  37.8 0.1 copy.17
  37.9 0.1 squeeze.12
  38.0 0.8 gather_fusion
  38.9 0.2 multiply_convert_fusion
  39.0 0.2 reshape.55
  39.2 17.6 %all_to_all.16 = bf16[16,2,7168]{2,1,0:T(2,128)(2,1)} all-to-all(bf16[16,2,7168]{2,1,0:T(2,128)(2,1)S(1)} %reshape.55), channel_id=1, replica_groups=mesh['group'=16,'blk'=16] {'group'}, dimensions={0} | all-to-all | bytes 917504 | tf_op jit(solution)/shard_map/all_to_all | solution.py:35
  56.9 149.3 %all-gather.7.cloned.1.call-done = bf16[256,2,7168]{2,1,0:T(2,128)(2,1)} async-done(((bf16[16,2,7168]{2,1,0:T(2,128)(2,1)}), bf16[256,2,7168]{2,1,0:T(2,128)(2,1)}) %all-gather.7.cloned.1.call-update) | async-done | bytes 7340048 | tf_op jit(solution)/shard_map/all_gather | solution.py:44
  206.1 15.4 %reshape.58 = bf16[512,7168]{1,0:T(8,128)(2,1)} reshape(bf16[256,2,7168]{2,1,0:T(2,128)(2,1)} %all-gather.7.cloned.1.call-done) | data formatting | bytes 14680064 | tf_op jit(solution)/shard_map/reshape | solution.py:47
  221.6 5.3 fusion.5
  226.9 0.4 copy-done.4
  227.3 2.1 fusion.8
  229.3 144.2 %all-gather.5.cloned.1.call-done = bf16[256,2,7168]{2,1,0:T(2,128)(2,1)} async-done(((bf16[16,2,7168]{2,1,0:T(2,128)(2,1)}), bf16[256,2,7168]{2,1,0:T(2,128)(2,1)}) %all-gather.5.cloned.1.call-update) | async-done | bytes 7340048 | tf_op jit(solution)/shard_map/all_gather | solution.py:45
  373.5 15.4 %reshape.56 = bf16[512,7168]{1,0:T(8,128)(2,1)} reshape(bf16[256,2,7168]{2,1,0:T(2,128)(2,1)} %all-gather.5.cloned.1.call-done) | data formatting | bytes 14680064 | tf_op jit(solution)/shard_map/reshape | solution.py:48
  388.9 5.6 multiply_convert_fusion.2
  394.6 7.3 %fusion.3 = f32[512,7168]{1,0:T(8,128)} fusion(bf16[512,128]{1,0:T(8,128)(2,1)S(1)} %get-tuple-element.6, bf16[1,7168,128]{2,1,0:T(8,128)(2,1)S(1)} %copy-done), kind=kOutput, calls=%fused_computation.10 | convolution fusion | flops 939524096 | bytes 16646144 | tf_op jit(solution)/shard_map/dot_general | solution.py:14
  401.9 10.2 %add_convert_fusion = bf16[512,7168]{1,0:T(8,128)(2,1)} fusion(f32[512,7168]{1,0:T(8,128)} %fusion.3, bf16[512,128]{1,0:T(8,128)(2,1)S(1)} %get-tuple-element.5, bf16[1,7168,128]{2,1,0:T(8,128)(2,1)S(1)} %copy-done.5), kind=kOutput, calls=%fused_computation.2 | convolution fusion | flops 946864128 | bytes 23986176 | tf_op jit(solution)/shard_map/dot_general | solution.py:14
  412.1 6.4 %fusion.1 = bf16[1,7168,128]{2,1,0:T(8,128)(2,1)} fusion(bf16[512,7168]{1,0:T(8,128)(2,1)} %reshape.58, bf16[512,128]{1,0:T(8,128)(2,1)S(1)} %get-tuple-element.5), kind=kOutput, calls=%fused_computation.7 | convolution fusion | flops 940441600 | bytes 9306112 | tf_op jit(solution)/shard_map/dot_general | solution.py:8
  418.5 156.4 %reduce-scatter.2.cloned.1.call-done = bf16[1,32,7168]{2,1,0:T(8,128)(2,1)} async-done(((bf16[16,32,7168]{2,1,0:T(8,128)(2,1)}), bf16[1,32,7168]{2,1,0:T(8,128)(2,1)}) %reduce-scatter.2.cloned.1.call-update) | async-done | bytes 458768 | tf_op jit(solution)/shard_map/reduce_scatter | solution.py:66
  574.9 2.0 convert_element_type.44
  576.9 7.8 %all-to-all-start.2 = ((bf16[16,2,7168]{2,1,0:T(2,128)(2,1)}), bf16[16,2,7168]{2,1,0:T(2,128)(2,1)S(1)}, u32[]{:S(2)}, u32[]{:S(2)}) async-start(bf16[16,2,7168]{2,1,0:T(2,128)(2,1)} %convert_element_type.44), calls=%async_computation.3 | async-start | bytes 917504 | tf_op jit(solution)/shard_map/all_to_all | solution.py:72
  584.7 5.7 fusion.2
  590.4 6.4 %fusion = bf16[1,7168,128]{2,1,0:T(8,128)(2,1)} fusion(bf16[512,7168]{1,0:T(8,128)(2,1)} %reshape.58, bf16[512,128]{1,0:T(8,128)(2,1)S(1)} %get-tuple-element.6), kind=kOutput, calls=%fused_computation.6 | convolution fusion | flops 940441600 | bytes 9306112 | tf_op jit(solution)/shard_map/dot_general | solution.py:8
  596.8 2.7 all-to-all-done.2
  599.5 0.2 reshape.60
  599.7 1.2 convolution_convert_fusion.3
  (26 shorter events, 0.3 us)
Async XLA Ops:
  7.2 214.4 %copy-start = (bf16[1,7168,128]{2,1,0:T(8,128)(2,1)S(1)}, bf16[1,7168,128]{2,1,0:T(8,128)(2,1)}, u32[]{:S(2)}) copy-start(bf16[1,7168,128]{2,1,0:T(8,128)(2,1)} %param.12) | copy-start | bytes 5505028
  7.2 30.5 %copy-start.7 = (s32[1,16]{1,0:T(1,128)S(1)}, s32[1,16]{1,0:T(1,128)}, u32[]{:S(2)}) copy-start(s32[1,16]{1,0:T(1,128)} %param.16) | copy-start | bytes 196
  7.2 30.6 %copy-start.6 = (f32[1,16,2]{1,2,0:T(2,128)S(1)}, f32[1,16,2]{1,2,0:T(2,128)}, u32[]{:S(2)}) copy-start(f32[1,16,2]{1,2,0:T(2,128)} %param.15) | copy-start | bytes 388
  7.2 30.8 %copy-start.3 = (bf16[48,7168]{1,0:T(8,128)(2,1)S(1)}, bf16[48,7168]{1,0:T(8,128)(2,1)}, u32[]{:S(2)}) copy-start(bf16[48,7168]{1,0:T(8,128)(2,1)} %param.11) | copy-start | bytes 2064388
  7.2 198.9 %all-gather.7.cloned.1.call-start = ((), (), s32[]{:S(2)}) async-start(), calls=%async_computation.6 | async-start | bytes 7798784 | tf_op jit(solution)/shard_map/all_gather | solution.py:44
  37.6 335.9 %all-gather.5.cloned.1.call-start = ((), (), s32[]{:S(2)}) async-start(), calls=%async_computation.5 | async-start | bytes 7798784 | tf_op jit(solution)/shard_map/all_gather | solution.py:45
  56.8 518.1 %reduce-scatter.2.cloned.1.call-start = ((), (), s32[]{:S(2)}) async-start(), calls=%async_computation.4 | async-start | bytes 7798784 | tf_op jit(solution)/shard_map/reduce_scatter | solution.py:66
  221.6 5.3 copy-start.2
  221.6 5.7 copy-start.4
  394.6 7.3 %copy-start.5 = (bf16[1,7168,128]{2,1,0:T(8,128)(2,1)S(1)}, bf16[1,7168,128]{2,1,0:T(8,128)(2,1)}, u32[]{:S(2)}) copy-start(bf16[1,7168,128]{2,1,0:T(8,128)(2,1)} %param.13) | copy-start | bytes 5505028
  576.9 22.6 %all-to-all-start.2 = ((bf16[16,2,7168]{2,1,0:T(2,128)(2,1)}), bf16[16,2,7168]{2,1,0:T(2,128)(2,1)S(1)}, u32[]{:S(2)}, u32[]{:S(2)}) async-start(bf16[16,2,7168]{2,1,0:T(2,128)(2,1)} %convert_element_type.44), calls=%async_computation.3 | async-start | bytes 917504 | tf_op jit(solution)/shard_map/all_to_all | solution.py:72
  584.7 16.1 %copy-start.1 = (bf16[1,7168,128]{2,1,0:T(8,128)(2,1)S(1)}, bf16[1,7168,128]{2,1,0:T(8,128)(2,1)}, u32[]{:S(2)}) copy-start(bf16[1,7168,128]{2,1,0:T(8,128)(2,1)} %param.12) | copy-start | bytes 5505028
Sparse Core Ops, SparseCore 0:
  37.7 168.3 all-gather.6
  207.9 165.5 all-gather.4
  412.2 162.6 reduce-scatter.1
where the time goes:
time: 609 us; the launch traced here: 607 us
  waiting for transfers between devices  453 us (74%)
  matrix products  50.2 us (8%)
  blocking collectives  44.1 us (7%)
  local copies, waits for them, and re-layouts  38.3 us (6%)
  between operations  13.9 us (2%)
  starting transfers between devices  7.96 us (1%)
    reduce_scatter x1, waiting for transfers between devices, body(): lax.psum_scatter(partial_value.astype(jnp.float32).astype(jnp.bfloat16),...  156 us
    all_gather x1, waiting for transfers between devices, body(): piece_in = lax.all_gather(recv_in[None], 'blk', axis=0, tiled=True)  149 us
    all_gather x1, waiting for transfers between devices, body(): piece_scaled = lax.all_gather(recv_scaled[None], 'blk', axis=0, tiled=True)  144 us
    all_to_all x1, blocking collectives, body(): lax.all_to_all(rows_in.reshape(experts, cap, width), 'group', split_axis=...  26.5 us
    dot_general x3, matrix products, contract_cols(): lax.dot_general(left, right, (((1,), (1,)), ((), ())), preferred_element_...  23.1 us
    dot_general x3, matrix products, contract_rows(): lax.dot_general(left, right, (((0,), (0,)), ((), ())), preferred_element_...  18.6 us
    all_to_all x1, blocking collectives, body(): lax.all_to_all(scaled.reshape(experts, cap, width), 'group', split_axis=0...  17.6 us
    reshape x1, local copies, waits for them, and re-layouts, body(): flat_in = piece_in.reshape(count * per_block, width)  15.4 us
  transfers between devices with their start and end apart: 4, of which 4 were waited for; matrix products, arithmetic and copies ran while one was open for 7% of the time, Pallas kernels for 0%

commit v1 on v0

v1 whole, which is shorter than its diff:
```python
import functools

import jax
import jax.numpy as jnp
from jax import lax
from jax.experimental import pallas as pl
from jax.experimental.pallas import tpu as pltpu
from jax.sharding import PartitionSpec as P

MESH = pl.DeviceIdType.MESH
NX, NY, NZ, NC, RUN = 4, 4, 8, 2, 4
Q = 4
HOPS = (0, 1, 7, 2, 6, 3, 5, 4)


def contract_rows(left, right):
    return lax.dot_general(
        left, right, (((0,), (0,)), ((), ())), preferred_element_type=jnp.float32
    )


def contract_cols(left, right):
    return lax.dot_general(
        left, right, (((1,), (1,)), ((), ())), preferred_element_type=jnp.float32
    )


def place():
    group, blk = lax.axis_index("group"), lax.axis_index("blk")
    x, z_hi, core = group // 4, (group // 2) % 2, group % 2
    y, z_lo = blk // RUN, blk % RUN
    return x, y, z_hi * RUN + z_lo, core


def device(x, y, z, core):
    return (x * 4 + (z // RUN) * 2 + core, y * RUN + z % RUN)


def x_peers(me):
    x, y, z, core = me
    for step in range(1, NX * NC):
        px, pc = (x + step // NC) % NX, (core + step % NC) % NC
        yield step - 1, px * NC + pc, device(px, y, z, pc)


def greet(me):
    x, y, z, core = me
    barrier = pltpu.get_barrier_semaphore()
    peers = [d for _, _, d in x_peers(me)]
    peers += [device(x, y, (z + hop) % NZ, core) for hop in range(1, NZ)]
    peers += [device(x, (y + 1) % NY, z, core), device(x, (y + 3) % NY, z, core)]
    for peer in peers:
        pl.semaphore_signal(barrier, inc=1, device_id=peer, device_id_type=MESH)
    pl.semaphore_wait(barrier, len(peers))


def remote(src, dst, send, recv, to):
    return pltpu.make_async_remote_copy(
        src_ref=src, dst_ref=dst, send_sem=send, recv_sem=recv, device_id=to, device_id_type=MESH
    )


def order_matrix():
    row = lax.broadcasted_iota(jnp.int32, (128, 128), 0)
    col = lax.broadcasted_iota(jnp.int32, (128, 128), 1)
    h, q, s, c = row // 64, (row // 16) % 4, (row // 2) % 8, row % 2
    return (col == s * 16 + h * 8 + c * 4 + q).astype(jnp.bfloat16)


def spread_kernel(
    tok_ref, cot_ref, pick_ref, scale_ref, out_in, out_sc,
    mess, recv, block, xs, xr, zs, zr, ys, yr, fs, fr, own_sem,
):
    me = place()
    x, y, z, core = me
    mine = x * NC + core
    width = tok_ref.shape[1] // Q
    half = tok_ref.shape[1] // 2
    outs = (out_in, out_sc)
    order = order_matrix()
    up, down = device(x, (y + 1) % NY, z, core), device(x, (y + 3) % NY, z, core)
    greet(me)

    def x_copy(t, i, slot, to):
        return remote(mess.at[t, slot], recv.at[t, mine], xs.at[t, i], xr.at[t, i], to)

    for t, rows_ref in enumerate((tok_ref, cot_ref)):
        total = jnp.zeros((128, width), jnp.float32)
        for q in range(Q):
            total = total + jnp.dot(
                pick_ref[q], rows_ref[:, q * width:(q + 1) * width],
                preferred_element_type=jnp.float32,
            )
        if t == 1:
            total = total * scale_ref[...]
        mess[t] = total.astype(jnp.bfloat16).reshape(8, 16, width)
        for i, slot, to in x_peers(me):
            x_copy(t, i, slot, to).start()
        recv[t, pl.ds(mine, 1)] = mess[t, pl.ds(mine, 1)]

    def z_copy(t, k):
        zt = (z + HOPS[k]) % NZ
        return remote(
            block.at[t, zt // RUN], outs[t].at[0, k], zs.at[t, k], zr.at[t, k],
            device(x, y, zt, core),
        )

    def y_copy(t, k, side, src=None):
        src = outs[t].at[0, k] if src is None else src
        return remote(
            src, outs[t].at[1 + side, k], ys.at[t, side, k], yr.at[t, side, k],
            down if side else up,
        )

    def f_copy(t, k, side):
        cols = pl.ds(side * half, half)
        return remote(
            outs[t].at[1 + side, k, :, cols], outs[t].at[3, k, :, cols],
            fs.at[t, side, k], fr.at[t, side, k], down if side else up,
        )

    def own_copy(t):
        return pltpu.make_async_copy(block.at[t, z // RUN], outs[t].at[0, 0], own_sem.at[t])

    for t in range(2):
        for i, slot, to in x_peers(me):
            x_copy(t, i, slot, to).wait_recv()
        rows = jnp.dot(
            order, recv[t].reshape(128, width), preferred_element_type=jnp.float32
        ).astype(jnp.bfloat16)
        for h in range(2):
            for q in range(Q):
                start = (h * Q + q) * 16
                block[t, h, :, q * width:(q + 1) * width] = rows[start:start + 16]
        for side in range(2):
            y_copy(t, 0, side, block.at[t, z // RUN]).start()
        for k in range(1, NZ):
            z_copy(t, k).start()
        own_copy(t).start()

    def forward(t, k):
        for side in range(2):
            y_copy(t, k, side).wait_recv()
            f_copy(t, k, side).start()

    for t in range(2):
        @pl.loop(1, NZ)
        def _(k, t=t):
            zt = z
            remote(
                block.at[t, 0], outs[t].at[0, k], zs.at[t, k], zr.at[t, k], (up[0], up[1])
            ).wait_recv()
            for side in range(2):
                y_copy(t, k, side).start()
            forward(t, k - 1)

    for t in range(2):
        forward(t, NZ - 1)
    for t in range(2):
        own_copy(t).wait()
        for i, slot, to in x_peers(me):
            x_copy(t, i, slot, to).wait_send()

        @pl.loop(0, NZ)
        def _(k, t=t):
            for side in range(2):
                y_copy(t, k, side).wait_send()
                f_copy(t, k, side).wait()

        for k in range(1, NZ):
            z_copy(t, k).wait_send()


def spread(tokens, cotangent, pick, scale):
    dim = tokens.shape[1]
    out = jax.ShapeDtypeStruct((4, NZ, 16, dim), jnp.bfloat16)
    vmem = pl.BlockSpec(memory_space=pltpu.VMEM)
    dma = pltpu.SemaphoreType.DMA
    return pl.pallas_call(
        spread_kernel,
        out_shape=(out, out),
        in_specs=[vmem] * 4,
        out_specs=(pl.BlockSpec(memory_space=pl.ANY),) * 2,
        scratch_shapes=[
            pltpu.VMEM((2, 8, 16, dim // Q), jnp.bfloat16),
            pltpu.VMEM((2, 8, 16, dim // Q), jnp.bfloat16),
            pltpu.VMEM((2, 2, 16, dim), jnp.bfloat16),
            dma((2, 7)), dma((2, 7)), dma((2, NZ)), dma((2, NZ)),
            dma((2, 2, NZ)), dma((2, 2, NZ)), dma((2, 2, NZ)), dma((2, 2, NZ)), dma((2,)),
        ],
        compiler_params=pltpu.CompilerParams(
            collective_id=0, has_side_effects=True, vmem_limit_bytes=40 * 2**20
        ),
        name="spread",
    )(tokens, cotangent, pick, scale)


def collect_kernel(
    part, pick_ref, out_ref,
    half_in, stage, side_in, summed, z_in, mess, recv,
    hs, hr, ds, dr, ss, sr, zs, zr, xs, xr,
):
    me = place()
    x, y, z, core = me
    mine = x * NC + core
    dim = part.shape[-1]
    width, half = dim // Q, dim // 2
    order = order_matrix()
    up, down = device(x, (y + 1) % NY, z, core), device(x, (y + 3) % NY, z, core)
    greet(me)
    cols = (pl.ds(0, half), pl.ds(half, half))
    sides = (down, up)

    def h_copy(k, side):
        return remote(
            part.at[3, k, :, cols[side]], half_in.at[side, k],
            hs.at[side, k], hr.at[side, k], sides[side],
        )

    def d_copy(k, side):
        return remote(
            part.at[1 + side, k, :, cols[1 - side]], side_in.at[side, k, :, cols[1 - side]],
            ds.at[side, k], dr.at[side, k], sides[side],
        )

    def s_copy(k, side):
        return remote(
            stage.at[side, k], side_in.at[side, k, :, cols[side]],
            ss.at[side, k], sr.at[side, k], sides[side],
        )

    def z_copy(k):
        zt = (z + NZ - HOPS[k]) % NZ
        return remote(
            summed.at[k], z_in.at[z], zs.at[k], zr.at[k], device(x, y, zt, core)
        )

    @pl.loop(0, NZ)
    def _(k):
        for side in range(2):
            h_copy(k, side).start()
            d_copy(k, side).start()

    f32 = jnp.float32

    def relay(k):
        for side in range(2):
            h_copy(k, side).wait_recv()
            stage[side, k] = (
                half_in[side, k].astype(f32) + part[1 + side, k, :, cols[side]].astype(f32)
            ).astype(jnp.bfloat16)
            s_copy(k, side).start()

    def total(k):
        for side in range(2):
            d_copy(k, side).wait_recv()
            s_copy(k, side).wait_recv()
        return (
            part[0, k].astype(f32) + side_in[0, k].astype(f32) + side_in[1, k].astype(f32)
        ).astype(jnp.bfloat16)

    relay(0)
    for k in range(NZ):
        if k + 1 < NZ:
            relay(k + 1)
        if k == 0:
            z_in[pl.ds(z, 1)] = total(k)[None]
        else:
            summed[k] = total(k)
            z_copy(k).start()

    for k in range(1, NZ):
        z_copy(k).wait_recv()
    pieces = []
    for h in range(2):
        for q in range(Q):
            c = slice(q * width, (q + 1) * width)
            acc = z_in[h * RUN, :, c].astype(f32)
            for l in range(1, RUN):
                acc = acc + z_in[h * RUN + l, :, c].astype(f32)
            pieces.append(acc.astype(jnp.bfloat16))
    mess[...] = contract_rows(order, jnp.concatenate(pieces, axis=0)).astype(
        jnp.bfloat16
    ).reshape(8, 16, width)

    def x_copy(i, slot, to):
        return remote(mess.at[slot], recv.at[mine], xs.at[i], xr.at[i], to)

    for i, slot, to in x_peers(me):
        x_copy(i, slot, to).start()
    recv[pl.ds(mine, 1)] = mess[pl.ds(mine, 1)]
    for i, slot, to in x_peers(me):
        x_copy(i, slot, to).wait_recv()
    for q in range(Q):
        out_ref[:, q * width:(q + 1) * width] = contract_rows(
            pick_ref[q], recv[...].reshape(128, width)
        ).astype(jnp.bfloat16)

    for i, slot, to in x_peers(me):
        x_copy(i, slot, to).wait_send()

    @pl.loop(0, NZ)
    def _(k):
        for side in range(2):
            h_copy(k, side).wait_send()
            d_copy(k, side).wait_send()
            s_copy(k, side).wait_send()

    for k in range(1, NZ):
        z_copy(k).wait_send()


def collect(part, pick, tok_dev):
    dim = part.shape[-1]
    vmem = pl.BlockSpec(memory_space=pltpu.VMEM)
    dma = pltpu.SemaphoreType.DMA
    bf = jnp.bfloat16
    pair = dma((2, NZ))
    return pl.pallas_call(
        collect_kernel,
        out_shape=jax.ShapeDtypeStruct((tok_dev, dim), bf),
        in_specs=[vmem] * 2,
        out_specs=vmem,
        scratch_shapes=[
            pltpu.VMEM((2, NZ, 16, dim // 2), bf),
            pltpu.VMEM((2, NZ, 16, dim // 2), bf),
            pltpu.VMEM((2, NZ, 16, dim), bf),
            pltpu.VMEM((NZ, 16, dim), bf),
            pltpu.VMEM((NZ, 16, dim), bf),
            pltpu.VMEM((8, 16, dim // Q), bf),
            pltpu.VMEM((8, 16, dim // Q), bf),
            pair, pair, pair, pair, pair, pair,
            dma((NZ,)), dma((NZ,)), dma((7,)), dma((7,)),
        ],
        compiler_params=pltpu.CompilerParams(
            collective_id=1, has_side_effects=True, vmem_limit_bytes=48 * 2**20
        ),
        name="collect",
    )(part, pick)


def body(tokens, cotangent, w_gate, w_up, w_down, gate_weight, counts, slots):
    experts = counts.shape[1]
    cap = slots.shape[2]
    tok_dev = tokens.shape[0]
    width = tokens.shape[1]
    position = lax.broadcasted_iota(jnp.int32, (experts, cap), 1)
    live = jnp.where(position < counts[0][:, None], gate_weight[0], jnp.zeros_like(gate_weight[0]))

    def rows(a):
        a = a.reshape(NX, 2, NC, cap).transpose(0, 2, 1, 3).reshape(experts * cap, 1)
        return jnp.broadcast_to(a, (experts * cap, Q)).reshape(experts * cap * Q, 1)

    slot_rows = rows(slots[0])
    dims = (Q, experts * cap * Q, tok_dev)
    pick = (
        (slot_rows[None] == lax.broadcasted_iota(jnp.int32, dims, 2))
        & (lax.broadcasted_iota(jnp.int32, dims, 1) % Q == lax.broadcasted_iota(jnp.int32, dims, 0))
    ).astype(jnp.bfloat16)
    got_in, got_scaled = spread(tokens, cotangent, pick, rows(live))
    flat_in = got_in.reshape(-1, width)
    flat_scaled = got_scaled.reshape(-1, width)
    gate_mat, up_mat, down_mat = w_gate[0], w_up[0], w_down[0]
    pre_gate = jnp.dot(flat_in, gate_mat, preferred_element_type=jnp.float32)
    pre_up = jnp.dot(flat_in, up_mat, preferred_element_type=jnp.float32)
    sigma = jax.nn.sigmoid(pre_gate)
    silu_val = pre_gate * sigma
    act = (silu_val * pre_up).astype(jnp.bfloat16)
    grad_hidden = contract_cols(flat_scaled, down_mat)
    grad_pre_gate = (grad_hidden * pre_up * sigma * (1.0 + pre_gate * (1.0 - sigma))).astype(
        jnp.bfloat16
    )
    grad_pre_up = (grad_hidden * silu_val).astype(jnp.bfloat16)
    acc_gate = contract_rows(flat_in, grad_pre_gate)
    acc_up = contract_rows(flat_in, grad_pre_up)
    acc_down = contract_rows(act, flat_scaled)
    part = contract_cols(grad_pre_gate, gate_mat) + contract_cols(grad_pre_up, up_mat)
    part = part.astype(jnp.bfloat16).reshape(4, NZ, 16, width)
    grad_tokens = collect(part, pick, tok_dev)
    return (
        grad_tokens,
        acc_gate.astype(jnp.bfloat16)[None],
        acc_up.astype(jnp.bfloat16)[None],
        acc_down.astype(jnp.bfloat16)[None],
    )


def solution(mesh):
    in_specs = (
        P(("group", "blk"), None),
        P(("group", "blk"), None),
        P("group", None, "blk"),
        P("group", None, "blk"),
        P("group", "blk", None),
        P(("group", "blk"), None, None),
        P(("group", "blk"), None),
        P(("group", "blk"), None, None),
    )
    out_specs = (
        P(("group", "blk"), None),
        P("group", None, "blk"),
        P("group", None, "blk"),
        P("group", "blk", None),
    )
    return jax.shard_map(body, mesh=mesh, in_specs=in_specs, out_specs=out_specs, check_vma=False)
```

time: 609 us -> 287 us (0.47)
  waiting for transfers between devices: 453 us -> 0 us
  Pallas kernels: 0 us -> 245 us
  blocking collectives: 44.1 us -> 0 us
  local copies, waits for them, and re-layouts: 38.3 us -> 5.99 us
  matrix products: 50.2 us -> 33.1 us
  between operations: 13.9 us -> 0.79 us
  starting transfers between devices: 7.96 us -> 0 us
    all_gather x2 -> x0, waiting for transfers between devices: 293 us -> none  [the longest x1 149 us: body(): piece_in = lax.all_gather(recv_in[None], 'blk', axis=0, tiled=True)]
    pallas_call x0 -> x2, Pallas kernels: none -> 245 us  [the longest x1 142 us: spread(): pl.pallas_call(spread_kernel, out_shape=(out, out), in_specs=[vmem] * 4,...]
    reduce_scatter x1 -> x0, waiting for transfers between devices: 156 us -> none  [body(): lax.psum_scatter(partial_value.astype(jnp.float32).astype(jnp.bfloat16),...]
    all_to_all x2 -> x0, blocking collectives: 44.1 us -> none  [the longest x1 26.5 us: body(): lax.all_to_all(rows_in.reshape(experts, cap, width), 'group', split_axis=...]
    reshape x5 -> x1, local copies, waits for them, and re-layouts: 31.4 us -> 0.08 us  [rows(): return jnp.broadcast_to(a, (experts * cap, Q)).reshape(experts * cap * Q, 1)]
    dot_general x3, matrix products: 18.6 us -> 9.23 us  [contract_rows(): lax.dot_general(left, right, (((0,), (0,)), ((), ())), preferred_element_...]
    all_to_all x1 -> x0, starting transfers between devices: 7.84 us -> none  [body(): lax.all_to_all(summed.reshape(groups, cap, width).astype(jnp.bfloat16), '...]
  transfers between devices with their start and end apart: 4 -> 0, of which waited for: 4 -> 0; matrix products, arithmetic and copies ran while one was open for 7% -> 0% of each run, Pallas kernels for 0% -> 0%
where the time goes in v1:
time: 287 us; the launch traced here: 286 us
  Pallas kernels  245 us (85%)
  matrix products  33.1 us (12%)
  local copies, waits for them, and re-layouts  5.99 us (2%)
    pallas_call x1, Pallas kernels, spread(): pl.pallas_call(spread_kernel, out_shape=(out, out), in_specs=[vmem] * 4,...  142 us
    pallas_call x1, Pallas kernels, collect(): pl.pallas_call(collect_kernel, out_shape=jax.ShapeDtypeStruct((tok_dev, d...  103 us
    dot_general x3, matrix products, contract_cols(): lax.dot_general(left, right, (((1,), (1,)), ((), ())), preferred_element_...  19.8 us
    dot_general x3, matrix products, contract_rows(): lax.dot_general(left, right, (((0,), (0,)), ((), ())), preferred_element_...  9.23 us

profile of v1, /device:TPU:1, one launch (start us, length us, event | category | flops | bytes accessed | tf_op | source)
XLA Modules:
  0.0 286.0 jit_solution(86578427614236635)
XLA Ops:
  0.6 0.0 copy-start
  0.6 0.5 broadcast.31
  1.2 1.4 reduce.3
  2.5 0.1 lt.18
  2.6 0.8 squeeze.12
  3.4 0.1 copy.16
  3.5 0.1 broadcast_in_dim.29
  3.6 0.8 reshape_squeeze.3
  4.4 0.1 copy.15
  4.5 0.1 broadcast_in_dim.26
  4.6 0.1 broadcast_in_dim.27
  4.7 0.1 eq.15
  4.8 0.1 broadcast_in_dim.30
  4.9 0.1 reshape.38.scale_ref
  5.0 0.1 fusion.14.pick_ref
  5.1 0.0 copy-start.1
  5.1 1.1 copy-done.1
  6.2 1.1 copy-done.2
  7.3 141.8 %spread.1 = (bf16[4,8,16,7168]{3,2,1,0:T(8,128)(2,1)S(1)}, bf16[4,8,16,7168]{3,2,1,0:T(8,128)(2,1)}) custom-call(bf16[48,7168]{1,0:T(8,128)(2,1)S(1)} %copy-done.1, bf16[48,7168]{1,0:T(8,128)(2,1)S(1)} %copy-done.2, bf16[4,128,48]{2,1,0:T(8,128)(2,1)S(1)} %fusion.14.pick_ref, f32[128,1]{1,0:T(8,128)S(1)} %reshape.38.scale_ref), custom_call_target="tpu_custom_call" | custom-call | tf_op jit(solution)/shard_map/spread/pallas_call | solution.py:179
  149.2 0.0 slice-start
  149.2 0.0 copy-start.4
  149.2 2.1 fusion.5
  151.3 0.0 slice-start.1
  151.3 2.1 fusion.8
  153.4 2.1 multiply_convert_fusion.1
  155.5 2.5 fusion.2
  158.0 3.4 %fusion.1 = bf16[1,7168,128]{2,1,0:T(8,128)(2,1)} fusion(bf16[512,7168]{1,0:T(8,128)(2,1)S(1)} %bitcast.43, bf16[512,128]{1,0:T(8,128)(2,1)S(1)} %get-tuple-element.8), kind=kOutput, calls=%fused_computation.5 | convolution fusion | flops 940441600 | bytes 9306112 | tf_op jit(solution)/shard_map/dot_general | solution.py:17
  161.4 3.4 %fusion = bf16[1,7168,128]{2,1,0:T(8,128)(2,1)} fusion(bf16[512,7168]{1,0:T(8,128)(2,1)S(1)} %bitcast.44, bf16[512,128]{1,0:T(8,128)(2,1)S(1)} %get-tuple-element.9), kind=kOutput, calls=%fused_computation.4 | convolution fusion | flops 940441600 | bytes 9306112 | tf_op jit(solution)/shard_map/dot_general | solution.py:17
  164.7 7.5 %fusion.3 = f32[512,7168]{1,0:T(8,128)} fusion(bf16[512,128]{1,0:T(8,128)(2,1)S(1)} %get-tuple-element.9, bf16[1,7168,128]{2,1,0:T(8,128)(2,1)S(1)} %copy-done), kind=kOutput, calls=%fused_computation.7 | convolution fusion | flops 939524096 | bytes 16646144 | tf_op jit(solution)/shard_map/dot_general | solution.py:23
  172.2 10.2 %add_convert_fusion = bf16[512,7168]{1,0:T(8,128)(2,1)} fusion(f32[512,7168]{1,0:T(8,128)} %fusion.3, bf16[512,128]{1,0:T(8,128)(2,1)S(1)} %get-tuple-element.8, bf16[1,7168,128]{2,1,0:T(8,128)(2,1)S(1)} %copy-done.3), kind=kOutput, calls=%fused_computation | convolution fusion | flops 946864128 | bytes 23986176 | tf_op jit(solution)/shard_map/dot_general | solution.py:23
  182.4 102.7 %collect.1 = bf16[48,7168]{1,0:T(8,128)(2,1)S(1)} custom-call(bf16[4,8,16,7168]{3,2,1,0:T(8,128)(2,1)} %bitcast.45, bf16[4,128,48]{2,1,0:T(8,128)(2,1)S(1)} %fusion.14.pick_ref), custom_call_target="tpu_custom_call" | custom-call | tf_op jit(solution)/shard_map/collect/pallas_call | solution.py:319
  285.1 0.8 copy.19
  (11 shorter events, 0.0 us)
Async XLA Ops:
  0.6 148.5 %copy-start = (bf16[1,7168,128]{2,1,0:T(8,128)(2,1)S(1)}, bf16[1,7168,128]{2,1,0:T(8,128)(2,1)}, u32[]{:S(2)}) copy-start(bf16[1,7168,128]{2,1,0:T(8,128)(2,1)} %param.10) | copy-start | bytes 5505028
  5.1 1.1 copy-start.1
  6.2 1.1 copy-start.2
  7.3 144.0 %copy-start.3 = (bf16[1,7168,128]{2,1,0:T(8,128)(2,1)S(1)}, bf16[1,7168,128]{2,1,0:T(8,128)(2,1)}, u32[]{:S(2)}) copy-start(bf16[1,7168,128]{2,1,0:T(8,128)(2,1)} %param.11) | copy-start | bytes 5505028
  149.2 4.2 %slice-start = ((s8[7340032]{0:T(1024)(128)(4,1)}), s8[4194304]{0:T(1024)(128)(4,1)S(1)}, s32[]{:S(2)}) async-start(s8[7340032]{0:T(1024)(128)(4,1)} %bitcast.46), calls=%async_computation | async-start | bytes 8388608
  149.2 4.2 %copy-start.4 = (bf16[1,128,7168]{2,1,0:T(8,128)(2,1)S(1)}, bf16[1,128,7168]{2,1,0:T(8,128)(2,1)}, u32[]{:S(2)}) copy-start(bf16[1,128,7168]{2,1,0:T(8,128)(2,1)} %param.12) | copy-start | bytes 5505028
  151.3 2.1 slice-start.1

commit v2 on v1

--- a/solution.py
+++ b/solution.py
@@ -146,10 +146,7 @@
     for t in range(2):
         @pl.loop(1, NZ)
         def _(k, t=t):
-            zt = z
-            remote(
-                block.at[t, 0], outs[t].at[0, k], zs.at[t, k], zr.at[t, k], (up[0], up[1])
-            ).wait_recv()
+            remote(block.at[t, 0], outs[t].at[0, k], zs.at[t, k], zr.at[t, k], up).wait_recv()
             for side in range(2):
                 y_copy(t, k, side).start()
             forward(t, k - 1)
@@ -235,15 +232,15 @@
             summed.at[k], z_in.at[z], zs.at[k], zr.at[k], device(x, y, zt, core)
         )
 
-    @pl.loop(0, NZ)
-    def _(k):
+    f32 = jnp.float32
+
+    def first(k):
         for side in range(2):
             h_copy(k, side).start()
+
+    def relay(k):
+        for side in range(2):
             d_copy(k, side).start()
-
-    f32 = jnp.float32
-
-    def relay(k):
         for side in range(2):
             h_copy(k, side).wait_recv()
             stage[side, k] = (
@@ -259,15 +256,18 @@
             part[0, k].astype(f32) + side_in[0, k].astype(f32) + side_in[1, k].astype(f32)
         ).astype(jnp.bfloat16)
 
-    relay(0)
-    for k in range(NZ):
-        if k + 1 < NZ:
-            relay(k + 1)
-        if k == 0:
-            z_in[pl.ds(z, 1)] = total(k)[None]
-        else:
+    for k in (7, 6, 5):
+        first(k)
+    relay(7)
+    for k in range(NZ - 1, -1, -1):
+        if k >= 3:
+            first(k - 3)
+        if k > 0:
+            relay(k - 1)
             summed[k] = total(k)
             z_copy(k).start()
+        else:
+            z_in[pl.ds(z, 1)] = total(k)[None]
 
     for k in range(1, NZ):
         z_copy(k).wait_recv()

time: 287 us -> 260 us (0.906)
  Pallas kernels: 245 us -> 218 us
    pallas_call x1, Pallas kernels: 103 us -> 76.2 us  [collect(): pl.pallas_call(collect_kernel, out_shape=jax.ShapeDtypeStruct((tok_dev, d...]
where the time goes in v2:
time: 260 us; the launch traced here: 259 us
  Pallas kernels  218 us (84%)
  matrix products  33.1 us (13%)
  local copies, waits for them, and re-layouts  5.99 us (2%)
    pallas_call x1, Pallas kernels, spread(): pl.pallas_call(spread_kernel, out_shape=(out, out), in_specs=[vmem] * 4,...  142 us
    pallas_call x1, Pallas kernels, collect(): pl.pallas_call(collect_kernel, out_shape=jax.ShapeDtypeStruct((tok_dev, d...  76.2 us
    dot_general x3, matrix products, contract_cols(): lax.dot_general(left, right, (((1,), (1,)), ((), ())), preferred_element_...  19.8 us
    dot_general x3, matrix products, contract_rows(): lax.dot_general(left, right, (((0,), (0,)), ((), ())), preferred_element_...  9.23 us

profile of v2, /device:TPU:1, one launch (start us, length us, event | category | flops | bytes accessed | tf_op | source)
XLA Modules:
  0.0 259.4 jit_solution(5629553656942261150)
XLA Ops:
  0.6 0.0 copy-start
  0.6 0.5 broadcast.31
  1.2 1.4 reduce.3
  2.5 0.1 lt.18
  2.6 0.8 squeeze.12
  3.4 0.1 copy.16
  3.5 0.1 broadcast_in_dim.29
  3.6 0.8 reshape_squeeze.3
  4.4 0.1 copy.15
  4.5 0.1 broadcast_in_dim.26
  4.6 0.1 broadcast_in_dim.27
  4.7 0.1 eq.15
  4.8 0.1 broadcast_in_dim.30
  4.9 0.1 reshape.38.scale_ref
  5.0 0.1 fusion.14.pick_ref
  5.1 0.0 copy-start.1
  5.1 1.1 copy-done.1
  6.2 1.1 copy-done.2
  7.3 141.8 %spread.1 = (bf16[4,8,16,7168]{3,2,1,0:T(8,128)(2,1)S(1)}, bf16[4,8,16,7168]{3,2,1,0:T(8,128)(2,1)}) custom-call(bf16[48,7168]{1,0:T(8,128)(2,1)S(1)} %copy-done.1, bf16[48,7168]{1,0:T(8,128)(2,1)S(1)} %copy-done.2, bf16[4,128,48]{2,1,0:T(8,128)(2,1)S(1)} %fusion.14.pick_ref, f32[128,1]{1,0:T(8,128)S(1)} %reshape.38.scale_ref), custom_call_target="tpu_custom_call" | custom-call | tf_op jit(solution)/shard_map/spread/pallas_call | solution.py:176
  149.2 0.0 slice-start
  149.2 0.0 copy-start.4
  149.2 2.1 fusion.5
  151.3 0.0 slice-start.1
  151.3 2.1 fusion.8
  153.4 2.1 multiply_convert_fusion.1
  155.5 2.5 fusion.2
  158.0 3.4 %fusion.1 = bf16[1,7168,128]{2,1,0:T(8,128)(2,1)} fusion(bf16[512,7168]{1,0:T(8,128)(2,1)S(1)} %bitcast.43, bf16[512,128]{1,0:T(8,128)(2,1)S(1)} %get-tuple-element.8), kind=kOutput, calls=%fused_computation.5 | convolution fusion | flops 940441600 | bytes 9306112 | tf_op jit(solution)/shard_map/dot_general | solution.py:17
  161.4 3.4 %fusion = bf16[1,7168,128]{2,1,0:T(8,128)(2,1)} fusion(bf16[512,7168]{1,0:T(8,128)(2,1)S(1)} %bitcast.44, bf16[512,128]{1,0:T(8,128)(2,1)S(1)} %get-tuple-element.9), kind=kOutput, calls=%fused_computation.4 | convolution fusion | flops 940441600 | bytes 9306112 | tf_op jit(solution)/shard_map/dot_general | solution.py:17
  164.7 7.5 %fusion.3 = f32[512,7168]{1,0:T(8,128)} fusion(bf16[512,128]{1,0:T(8,128)(2,1)S(1)} %get-tuple-element.9, bf16[1,7168,128]{2,1,0:T(8,128)(2,1)S(1)} %copy-done), kind=kOutput, calls=%fused_computation.7 | convolution fusion | flops 939524096 | bytes 16646144 | tf_op jit(solution)/shard_map/dot_general | solution.py:23
  172.2 10.2 %add_convert_fusion = bf16[512,7168]{1,0:T(8,128)(2,1)} fusion(f32[512,7168]{1,0:T(8,128)} %fusion.3, bf16[512,128]{1,0:T(8,128)(2,1)S(1)} %get-tuple-element.8, bf16[1,7168,128]{2,1,0:T(8,128)(2,1)S(1)} %copy-done.3), kind=kOutput, calls=%fused_computation | convolution fusion | flops 946864128 | bytes 23986176 | tf_op jit(solution)/shard_map/dot_general | solution.py:23
  182.4 76.2 %collect.1 = bf16[48,7168]{1,0:T(8,128)(2,1)S(1)} custom-call(bf16[4,8,16,7168]{3,2,1,0:T(8,128)(2,1)} %bitcast.45, bf16[4,128,48]{2,1,0:T(8,128)(2,1)S(1)} %fusion.14.pick_ref), custom_call_target="tpu_custom_call" | custom-call | tf_op jit(solution)/shard_map/collect/pallas_call | solution.py:319
  258.6 0.8 copy.19
  (11 shorter events, 0.0 us)
Async XLA Ops:
  0.6 148.5 %copy-start = (bf16[1,7168,128]{2,1,0:T(8,128)(2,1)S(1)}, bf16[1,7168,128]{2,1,0:T(8,128)(2,1)}, u32[]{:S(2)}) copy-start(bf16[1,7168,128]{2,1,0:T(8,128)(2,1)} %param.10) | copy-start | bytes 5505028
  5.1 1.1 copy-start.1
  6.2 1.1 copy-start.2
  7.3 144.0 %copy-start.3 = (bf16[1,7168,128]{2,1,0:T(8,128)(2,1)S(1)}, bf16[1,7168,128]{2,1,0:T(8,128)(2,1)}, u32[]{:S(2)}) copy-start(bf16[1,7168,128]{2,1,0:T(8,128)(2,1)} %param.11) | copy-start | bytes 5505028
  149.2 4.2 %slice-start = ((s8[7340032]{0:T(1024)(128)(4,1)}), s8[4194304]{0:T(1024)(128)(4,1)S(1)}, s32[]{:S(2)}) async-start(s8[7340032]{0:T(1024)(128)(4,1)} %bitcast.46), calls=%async_computation | async-start | bytes 8388608
  149.2 4.2 %copy-start.4 = (bf16[1,128,7168]{2,1,0:T(8,128)(2,1)S(1)}, bf16[1,128,7168]{2,1,0:T(8,128)(2,1)}, u32[]{:S(2)}) copy-start(bf16[1,128,7168]{2,1,0:T(8,128)(2,1)} %param.12) | copy-start | bytes 5505028
  151.3 2.1 slice-start.1

commit v3 on v2

v3 whole, which is shorter than its diff:
```python
import jax
import jax.numpy as jnp
from jax import lax
from jax.experimental import pallas as pl
from jax.experimental.pallas import tpu as pltpu
from jax.sharding import PartitionSpec as P

MESH = pl.DeviceIdType.MESH
NX, NY, NZ, NC, RUN = 4, 4, 8, 2, 4
Q = 4
HOPS = (0, 1, 7, 2, 6, 3, 5, 4)


def contract_rows(left, right):
    return lax.dot_general(
        left, right, (((0,), (0,)), ((), ())), preferred_element_type=jnp.float32
    )


def contract_cols(left, right):
    return lax.dot_general(
        left, right, (((1,), (1,)), ((), ())), preferred_element_type=jnp.float32
    )


def place():
    group, blk = lax.axis_index("group"), lax.axis_index("blk")
    x, z_hi, core = group // 4, (group // 2) % 2, group % 2
    y, z_lo = blk // RUN, blk % RUN
    return x, y, z_hi * RUN + z_lo, core


def device(x, y, z, core):
    return (x * 4 + (z // RUN) * 2 + core, y * RUN + z % RUN)


def x_peers(me):
    x, y, z, core = me
    for step in range(1, NX * NC):
        px, pc = (x + step // NC) % NX, (core + step % NC) % NC
        yield step - 1, px * NC + pc, device(px, y, z, pc)


def greet(me):
    x, y, z, core = me
    barrier = pltpu.get_barrier_semaphore()
    peers = [d for _, _, d in x_peers(me)]
    peers += [device(x, y, (z + hop) % NZ, core) for hop in range(1, NZ)]
    peers += [device(x, (y + 1) % NY, z, core), device(x, (y + 3) % NY, z, core)]
    for peer in peers:
        pl.semaphore_signal(barrier, inc=1, device_id=peer, device_id_type=MESH)
    pl.semaphore_wait(barrier, len(peers))


def remote(src, dst, send, recv, to):
    return pltpu.make_async_remote_copy(
        src_ref=src, dst_ref=dst, send_sem=send, recv_sem=recv, device_id=to, device_id_type=MESH
    )


def order_matrix():
    row = lax.broadcasted_iota(jnp.int32, (128, 128), 0)
    col = lax.broadcasted_iota(jnp.int32, (128, 128), 1)
    h, q, s, c = row // 64, (row // 16) % 4, (row // 2) % 8, row % 2
    return (col == s * 16 + h * 8 + c * 4 + q).astype(jnp.bfloat16)


def kernel(
    tok_hbm, cot_hbm, gate_hbm, up_hbm, down_hbm, pick_ref, scale_ref,
    out_ref, gate_out, up_out, down_out,
    given, both, w_down, mess, recv, block, rows_in, rows_sc, pre, grad_hid, grads, act,
    part, half_in, side_in, z_in, back, back_in, g_gate, g_up, g_down,
    load_sem, own_sem, store_sem,
    xs, xr, zs, zr, ys, yr, fs, fr, hs, hr, ds, dr, ss, sr, bs, br, cs, cr,
):
    f32, bf = jnp.float32, jnp.bfloat16
    me = place()
    x, y, z, core = me
    mine = x * NC + core
    dim = given.shape[-1]
    width, half = dim // Q, dim // 2
    hid = w_down.shape[0]
    rows = (rows_in, rows_sc)
    order = order_matrix()
    up, down = device(x, (y + 1) % NY, z, core), device(x, (y + 3) % NY, z, core)
    cols = (pl.ds(0, half), pl.ds(half, half))

    loads = [
        pltpu.make_async_copy(src, dst, load_sem.at[i])
        for i, (src, dst) in enumerate((
            (tok_hbm, given.at[0]), (cot_hbm, given.at[1]),
            (gate_hbm, both.at[:, pl.ds(0, hid)]), (up_hbm, both.at[:, pl.ds(hid, hid)]),
            (down_hbm, w_down),
        ))
    ]
    for load in loads:
        load.start()
    greet(me)

    def x_copy(t, i, slot, to):
        return remote(mess.at[t, slot], recv.at[t, mine], xs.at[t, i], xr.at[t, i], to)

    for t in range(2):
        loads[t].wait()
        total = jnp.zeros((128, width), f32)
        for q in range(Q):
            total = total + jnp.dot(
                pick_ref[q], given[t, :, q * width:(q + 1) * width], preferred_element_type=f32
            )
        if t == 1:
            total = total * scale_ref[...]
        mess[t] = total.astype(bf).reshape(8, 16, width)
        for i, slot, to in x_peers(me):
            x_copy(t, i, slot, to).start()
        recv[t, pl.ds(mine, 1)] = mess[t, pl.ds(mine, 1)]

    def at(ref, j, k, *more):
        return ref.at[(k // 4, j, k % 4) + more]

    def z_copy(t, k):
        zt = (z + HOPS[k]) % NZ
        return remote(
            block.at[t, zt // RUN], at(rows[t], 0, k), zs.at[t, k], zr.at[t, k],
            device(x, y, zt, core),
        )

    def y_copy(t, k, side):
        src = at(rows[t], 0, k) if k else block.at[t, z // RUN]
        return remote(
            src, at(rows[t], 1 + side, k), ys.at[t, side, k], yr.at[t, side, k],
            down if side else up,
        )

    def f_copy(t, k, side):
        c = (slice(None), cols[side])
        return remote(
            at(rows[t], 1 + side, k, *c), at(rows[t], 3, k, *c),
            fs.at[t, side, k], fr.at[t, side, k], down if side else up,
        )

    def own_copy(t):
        return pltpu.make_async_copy(block.at[t, z // RUN], at(rows[t], 0, 0), own_sem.at[t])

    for t in range(2):
        for i, slot, to in x_peers(me):
            x_copy(t, i, slot, to).wait_recv()
        moved = jnp.dot(
            order, recv[t].reshape(128, width), preferred_element_type=f32
        ).astype(bf)
        for h in range(2):
            for q in range(Q):
                start = (h * Q + q) * 16
                block[t, h, :, q * width:(q + 1) * width] = moved[start:start + 16]
        for side in range(2):
            y_copy(t, 0, side).start()
        for k in range(1, 4):
            z_copy(t, k).start()
        own_copy(t).start()
    for t in range(2):
        for k in range(4, NZ):
            z_copy(t, k).start()

    def arrived(t, hf):
        if hf == 0:
            own_copy(t).wait()
        for k in range(4 * hf, 4 * hf + 4):
            for side in range(2):
                f_copy(t, k, side).wait_recv()

    def chunk(c, size):
        return pl.ds(pl.multiple_of(c * size, size), size)

    def pre_acts(hf):
        pre[...] = jnp.zeros_like(pre)

        @pl.loop(0, dim // 1024)
        def _(c):
            cc = chunk(c, 1024)
            pre[...] += jnp.dot(
                rows_in[hf, :, :, :, cc].reshape(256, 1024), both[cc, :], preferred_element_type=f32
            )

    def hidden(hf):
        grad_hid[...] = jnp.zeros_like(grad_hid)

        @pl.loop(0, dim // 1024)
        def _(c):
            cc = chunk(c, 1024)
            grad_hid[...] += contract_cols(
                rows_sc[hf, :, :, :, cc].reshape(256, 1024), w_down[:, cc]
            )

        gate, lift, grad = pre[:, :hid], pre[:, hid:], grad_hid[...]
        sigma = jax.nn.sigmoid(gate)
        silu = gate * sigma
        act[hf] = (silu * lift).astype(bf)
        grads[hf, :, :hid] = (grad * lift * sigma * (1.0 + gate * (1.0 - sigma))).astype(bf)
        grads[hf, :, hid:] = (grad * silu).astype(bf)

    def parts(hf, lo, hi):
        @pl.loop(lo, hi)
        def _(c):
            cc = chunk(c, 512)
            part[hf, :, :, :, cc] = contract_cols(grads[hf], both[cc, :]).astype(bf).reshape(
                4, 4, 16, 512
            )

    def forward(t, k):
        for side in range(2):
            y_copy(t, k, side).wait_recv()
            f_copy(t, k, side).start()

    units = [(t, k) for hf in range(2) for t in range(2) for k in range(4 * hf, 4 * hf + 4)]
    for load in loads[2:]:
        load.wait()
    for i, (t, k) in enumerate(units):
        if k:
            z_copy(t, k).wait_recv()
            for side in range(2):
                y_copy(t, k, side).start()
        if i:
            forward(*units[i - 1])
        if i == 9:
            arrived(0, 0)
            pre_acts(0)
        if i == 11:
            arrived(1, 0)
            hidden(0)
        if i == 12:
            parts(0, 0, 7)
        if i == 13:
            parts(0, 7, 14)
    forward(*units[-1])

    sides = (down, up)

    def h_copy(k, side):
        return remote(
            at(part, 3, k, slice(None), cols[side]), half_in.at[side, k],
            hs.at[side, k], hr.at[side, k], sides[side],
        )

    def d_copy(k, side):
        return remote(
            at(part, 1 + side, k, slice(None), cols[1 - side]), side_in.at[side, k, :, cols[1 - side]],
            ds.at[side, k], dr.at[side, k], sides[side],
        )

    def s_copy(k, side):
        return remote(
            at(part, 1 + side, k, slice(None), cols[side]), side_in.at[side, k, :, cols[side]],
            ss.at[side, k], sr.at[side, k], sides[side],
        )

    def b_copy(k):
        zt = (z + NZ - HOPS[k]) % NZ
        return remote(at(part, 0, k), z_in.at[z], bs.at[k], br.at[k], device(x, y, zt, core))

    def first(k):
        for side in range(2):
            h_copy(k, side).start()

    def direct(k):
        for side in range(2):
            d_copy(k, side).start()

    def relay(k):
        for side in range(2):
            h_copy(k, side).wait_recv()
            own = part[k // 4, 1 + side, k % 4, :, cols[side]]
            part[k // 4, 1 + side, k % 4, :, cols[side]] = (
                half_in[side, k].astype(f32) + own.astype(f32)
            ).astype(bf)
            s_copy(k, side).start()

    def finish(k):
        for side in range(2):
            d_copy(k, side).wait_recv()
            s_copy(k, side).wait_recv()
        total = (
            part[k // 4, 0, k % 4].astype(f32) + side_in[0, k].astype(f32) + side_in[1, k].astype(f32)
        ).astype(bf)
        if k:
            part[k // 4, 0, k % 4] = total
            b_copy(k).start()
        else:
            z_in[pl.ds(z, 1)] = total[None]

    def weights_in(lo, hi):
        @pl.loop(lo, hi)
        def _(c):
            cc = chunk(c, 512)
            got = contract_rows(
                rows_in[:, :, :, :, cc].reshape(512, 512), grads[...].reshape(512, 2 * hid)
            ).astype(bf)
            g_gate[cc, :] = got[:, :hid]
            g_up[cc, :] = got[:, hid:]

    def weights_down(lo, hi):
        @pl.loop(lo, hi)
        def _(c):
            cc = chunk(c, 512)
            g_down[:, cc] = contract_rows(
                act[...].reshape(512, hid), rows_sc[:, :, :, :, cc].reshape(512, 512)
            ).astype(bf)

    stores = [
        pltpu.make_async_copy(src, dst, store_sem.at[i])
        for i, (src, dst) in enumerate(((g_gate, gate_out), (g_up, up_out), (g_down, down_out)))
    ]

    for k in (3, 2, 1, 0):
        first(k)
        direct(k)
    arrived(0, 1)
    pre_acts(1)
    arrived(1, 1)
    hidden(1)
    parts(1, 0, 14)
    for k in (3, 2, 1, 0):
        relay(k)
    for k in (7, 6, 5, 4):
        first(k)
        direct(k)
    weights_in(0, 7)
    for k in (3, 2):
        finish(k)
    weights_in(7, 14)
    for store in stores[:2]:
        store.start()
    for k in (1, 0):
        finish(k)
    for k in (7, 6, 5, 4):
        relay(k)
    weights_down(0, 14)
    stores[2].start()
    for k in (7, 6, 5, 4):
        finish(k)

    for k in range(1, NZ):
        b_copy(k).wait_recv()
    pieces = []
    for h in range(2):
        for q in range(Q):
            c = slice(q * width, (q + 1) * width)
            acc = z_in[h * RUN, :, c].astype(f32)
            for l in range(1, RUN):
                acc = acc + z_in[h * RUN + l, :, c].astype(f32)
            pieces.append(acc.astype(bf))
    back[...] = contract_rows(order, jnp.concatenate(pieces, axis=0)).astype(bf).reshape(8, 16, width)

    def c_copy(i, slot, to):
        return remote(back.at[slot], back_in.at[mine], cs.at[i], cr.at[i], to)

    for i, slot, to in x_peers(me):
        c_copy(i, slot, to).start()
    back_in[pl.ds(mine, 1)] = back[pl.ds(mine, 1)]
    for i, slot, to in x_peers(me):
        c_copy(i, slot, to).wait_recv()
    for q in range(Q):
        out_ref[:, q * width:(q + 1) * width] = contract_rows(
            pick_ref[q], back_in[...].reshape(128, width)
        ).astype(bf)

    for i, slot, to in x_peers(me):
        for t in range(2):
            x_copy(t, i, slot, to).wait_send()
        c_copy(i, slot, to).wait_send()
    for k in range(NZ):
        for side in range(2):
            for t in range(2):
                y_copy(t, k, side).wait_send()
                f_copy(t, k, side).wait_send()
            h_copy(k, side).wait_send()
            d_copy(k, side).wait_send()
            s_copy(k, side).wait_send()
        if k:
            for t in range(2):
                z_copy(t, k).wait_send()
            b_copy(k).wait_send()
    for store in stores:
        store.wait()


def experts_backward(tokens, cotangent, w_gate, w_up, w_down, pick, scale):
    dim, hid = w_gate.shape
    bf, f32 = jnp.bfloat16, jnp.float32
    vmem, hbm = pl.BlockSpec(memory_space=pltpu.VMEM), pl.BlockSpec(memory_space=pl.ANY)
    dma = pltpu.SemaphoreType.DMA
    message = pltpu.VMEM((8, 16, dim // Q), bf)
    side = dma((2, NZ))
    two_sides = dma((2, 2, NZ))
    return pl.pallas_call(
        kernel,
        out_shape=(
            jax.ShapeDtypeStruct(tokens.shape, bf),
            jax.ShapeDtypeStruct((dim, hid), bf),
            jax.ShapeDtypeStruct((dim, hid), bf),
            jax.ShapeDtypeStruct((hid, dim), bf),
        ),
        in_specs=[hbm] * 5 + [vmem] * 2,
        out_specs=(vmem, hbm, hbm, hbm),
        scratch_shapes=[
            pltpu.VMEM((2,) + tokens.shape, bf),
            pltpu.VMEM((dim, 2 * hid), bf),
            pltpu.VMEM((hid, dim), bf),
            pltpu.VMEM((2, 8, 16, dim // Q), bf),
            pltpu.VMEM((2, 8, 16, dim // Q), bf),
            pltpu.VMEM((2, 2, 16, dim), bf),
            pltpu.VMEM((2, 4, 4, 16, dim), bf),
            pltpu.VMEM((2, 4, 4, 16, dim), bf),
            pltpu.VMEM((256, 2 * hid), f32),
            pltpu.VMEM((256, hid), f32),
            pltpu.VMEM((2, 256, 2 * hid), bf),
            pltpu.VMEM((2, 256, hid), bf),
            pltpu.VMEM((2, 4, 4, 16, dim), bf),
            pltpu.VMEM((2, NZ, 16, dim // 2), bf),
            pltpu.VMEM((2, NZ, 16, dim), bf),
            pltpu.VMEM((NZ, 16, dim), bf),
            message, message,
            pltpu.VMEM((dim, hid), bf),
            pltpu.VMEM((dim, hid), bf),
            pltpu.VMEM((hid, dim), bf),
            dma((5,)), dma((2,)), dma((3,)),
            dma((2, 7)), dma((2, 7)), side, side,
            two_sides, two_sides, two_sides, two_sides,
            side, side, side, side, side, side,
            dma((NZ,)), dma((NZ,)), dma((7,)), dma((7,)),
        ],
        compiler_params=pltpu.CompilerParams(
            collective_id=0, has_side_effects=True, vmem_limit_bytes=62 * 2**20
        ),
        name="experts_backward",
    )(tokens, cotangent, w_gate, w_up, w_down, pick, scale)


def body(tokens, cotangent, w_gate, w_up, w_down, gate_weight, counts, slots):
    experts = counts.shape[1]
    cap = slots.shape[2]
    tok_dev = tokens.shape[0]
    position = lax.broadcasted_iota(jnp.int32, (experts, cap), 1)
    live = jnp.where(position < counts[0][:, None], gate_weight[0], jnp.zeros_like(gate_weight[0]))

    def rows(a):
        a = a.reshape(NX, 2, NC, cap).transpose(0, 2, 1, 3).reshape(experts * cap, 1)
        return jnp.broadcast_to(a, (experts * cap, Q)).reshape(experts * cap * Q, 1)

    slot_rows = rows(slots[0])
    dims = (Q, experts * cap * Q, tok_dev)
    pick = (
        (slot_rows[None] == lax.broadcasted_iota(jnp.int32, dims, 2))
        & (lax.broadcasted_iota(jnp.int32, dims, 1) % Q == lax.broadcasted_iota(jnp.int32, dims, 0))
    ).astype(jnp.bfloat16)
    grad_tokens, grad_gate, grad_up, grad_down = experts_backward(
        tokens, cotangent, w_gate[0], w_up[0], w_down[0], pick, rows(live)
    )
    return grad_tokens, grad_gate[None], grad_up[None], grad_down[None]


def solution(mesh):
    in_specs = (
        P(("group", "blk"), None),
        P(("group", "blk"), None),
        P("group", None, "blk"),
        P("group", None, "blk"),
        P("group", "blk", None),
        P(("group", "blk"), None, None),
        P(("group", "blk"), None),
        P(("group", "blk"), None, None),
    )
    out_specs = (
        P(("group", "blk"), None),
        P("group", None, "blk"),
        P("group", None, "blk"),
        P("group", "blk", None),
    )
    return jax.shard_map(body, mesh=mesh, in_specs=in_specs, out_specs=out_specs, check_vma=False)
```

time: 260 us -> 255 us (0.981); the launches traced: 259 us -> 251 us
  matrix products: 33.1 us -> 0 us
  Pallas kernels: 218 us -> 236 us
  local copies, waits for them, and re-layouts: 5.99 us -> 11.9 us
    dot_general x8 -> x0, matrix products: 33.1 us -> none  [the longest x3 19.8 us: contract_cols(): lax.dot_general(left, right, (((1,), (1,)), ((), ())), preferred_element_...]
    pallas_call x2 -> x1, Pallas kernels: 218 us -> 236 us  [experts_backward(): pl.pallas_call(kernel, out_shape=(jax.ShapeDtypeStruct(tokens.shape, bf),...]
    unnamed x16 -> x9, local copies, waits for them, and re-layouts: 3.58 us -> 8.88 us
where the time goes in v3:
time: 255 us; the launch traced here: 251 us
  Pallas kernels  236 us (93%)
  local copies, waits for them, and re-layouts  11.9 us (5%)
    pallas_call x1, Pallas kernels, experts_backward(): pl.pallas_call(kernel, out_shape=(jax.ShapeDtypeStruct(tokens.shape, bf),...  236 us
    unnamed x9, local copies, waits for them, and re-layouts  8.88 us

profile of v3, /device:TPU:1, one launch (start us, length us, event | category | flops | bytes accessed | tf_op | source)
XLA Modules:
  0.0 251.1 jit_solution(4028482913499522779)
XLA Ops:
  0.6 0.5 broadcast.20
  1.1 1.3 reduce.3
  2.5 0.1 lt.18
  2.6 0.8 squeeze.15
  3.3 0.1 copy.16
  3.5 0.1 broadcast_in_dim.29
  3.6 0.8 reshape_squeeze.3
  4.3 0.1 copy.15
  4.5 0.1 broadcast_in_dim.26
  4.6 0.1 broadcast_in_dim.27
  4.6 0.1 eq.15
  4.8 0.1 broadcast_in_dim.30
  4.8 0.7 reshape.26.scale_ref
  5.5 0.8 fusion.1.pick_ref
  6.3 236.4 %experts_backward.1 = (bf16[48,7168]{1,0:T(8,128)(2,1)}, bf16[7168,128]{1,0:T(8,128)(2,1)}, bf16[7168,128]{1,0:T(8,128)(2,1)}, bf16[128,7168]{1,0:T(8,128)(2,1)}) custom-call(bf16[48,7168]{1,0:T(8,128)(2,1)} %tok_hbm.1, bf16[48,7168]{1,0:T(8,128)(2,1)} %cot_hbm.1, bf16[7168,128]{1,0:T(8,128)(2,1)} %bitcast.16, bf16[7168,128]{1,0:T(8,128)(2,1)} %bitcast.17, ...), custom_call_target="tpu_custom_call" | custom-call | tf_op jit(solution)/shard_map/experts_backward/pallas_call | solution.py:393
  242.7 2.0 copy.22
  244.7 0.0 copy-start.1
  244.7 3.0 %copy.23 = bf16[1,7168,128]{2,1,0:T(8,128)(2,1)} copy(bf16[1,7168,128]{2,1,0:T(8,128)(2,1)} %bitcast.15) | data formatting | bytes 3670016
  247.7 0.0 copy-done.1
  247.7 0.0 copy-start
  247.7 1.2 copy.24
  248.9 0.9 copy-done
  249.9 1.2 copy.25
  (3 shorter events, 0.0 us)
Async XLA Ops:
  244.7 3.0 %copy-start.1 = (bf16[7168,128]{1,0:T(8,128)(2,1)S(1)}, bf16[7168,128]{1,0:T(8,128)(2,1)}, u32[]{:S(2)}) copy-start(bf16[7168,128]{1,0:T(8,128)(2,1)} %get-tuple-element.10) | copy-start | bytes 5505028
  247.7 2.2 copy-start

commit v4 on v3

--- a/solution.py
+++ b/solution.py
@@ -8,7 +8,7 @@
 MESH = pl.DeviceIdType.MESH
 NX, NY, NZ, NC, RUN = 4, 4, 8, 2, 4
 Q = 4
-HOPS = (0, 1, 7, 2, 6, 3, 5, 4)
+HOPS = (0, 1, 5, 4, 7, 2, 6, 3)
 
 
 def contract_rows(left, right):
@@ -66,11 +66,11 @@
 
 
 def kernel(
-    tok_hbm, cot_hbm, gate_hbm, up_hbm, down_hbm, pick_ref, scale_ref,
-    out_ref, gate_out, up_out, down_out,
+    tok_hbm, cot_hbm, gate_hbm, up_hbm, down_hbm, weight_ref, count_ref, slot_ref,
+    out_ref, g_gate, g_up, g_down,
     given, both, w_down, mess, recv, block, rows_in, rows_sc, pre, grad_hid, grads, act,
-    part, half_in, side_in, z_in, back, back_in, g_gate, g_up, g_down,
-    load_sem, own_sem, store_sem,
+    part, half_in, side_in, z_in, back, back_in, pick_ref,
+    load_sem, own_sem,
     xs, xr, zs, zr, ys, yr, fs, fr, hs, hr, ds, dr, ss, sr, bs, br, cs, cr,
 ):
     f32, bf = jnp.float32, jnp.bfloat16
@@ -97,6 +97,28 @@
         load.start()
     greet(me)
 
+    shape = (128, slot_ref.shape[1])
+    row = lax.broadcasted_iota(jnp.int32, shape, 0)
+    here = lax.broadcasted_iota(jnp.int32, shape, 1) == (
+        row // 32 * 4 + row // 8 % 2 * 2 + row // 16 % 2
+    )
+    second = row // 4 % 2 == 1
+
+    def of_row(table):
+        value = jnp.where(second, table[1:2], table[0:1])
+        return jnp.sum(jnp.where(here, value, jnp.zeros_like(value)), axis=1, keepdims=True)
+
+    position = lax.broadcasted_iota(jnp.int32, weight_ref.shape, 0)
+    scale = of_row(
+        jnp.where(position < count_ref[...], weight_ref[...], jnp.zeros_like(weight_ref[...]))
+    )
+    slot_row = of_row(slot_ref[...].astype(f32))
+    spots = (128, given.shape[1])
+    wanted = slot_row == lax.broadcasted_iota(jnp.int32, spots, 1).astype(f32)
+    part_of_row = lax.broadcasted_iota(jnp.int32, spots, 0) % Q
+    for q in range(Q):
+        pick_ref[q] = (wanted & (part_of_row == q)).astype(f32).astype(bf)
+
     def x_copy(t, i, slot, to):
         return remote(mess.at[t, slot], recv.at[t, mine], xs.at[t, i], xr.at[t, i], to)
 
@@ -108,7 +130,7 @@
                 pick_ref[q], given[t, :, q * width:(q + 1) * width], preferred_element_type=f32
             )
         if t == 1:
-            total = total * scale_ref[...]
+            total = total * scale
         mess[t] = total.astype(bf).reshape(8, 16, width)
         for i, slot, to in x_peers(me):
             x_copy(t, i, slot, to).start()
@@ -304,11 +326,6 @@
                 act[...].reshape(512, hid), rows_sc[:, :, :, :, cc].reshape(512, 512)
             ).astype(bf)
 
-    stores = [
-        pltpu.make_async_copy(src, dst, store_sem.at[i])
-        for i, (src, dst) in enumerate(((g_gate, gate_out), (g_up, up_out), (g_down, down_out)))
-    ]
-
     for k in (3, 2, 1, 0):
         first(k)
         direct(k)
@@ -317,25 +334,36 @@
     arrived(1, 1)
     hidden(1)
     parts(1, 0, 14)
-    for k in (3, 2, 1, 0):
-        relay(k)
-    for k in (7, 6, 5, 4):
-        first(k)
-        direct(k)
-    weights_in(0, 7)
-    for k in (3, 2):
-        finish(k)
-    weights_in(7, 14)
-    for store in stores[:2]:
-        store.start()
-    for k in (1, 0):
-        finish(k)
-    for k in (7, 6, 5, 4):
-        relay(k)
+    relay(3)
+    relay(2)
+    first(7)
+    relay(1)
+    relay(0)
+    first(6)
+    direct(7)
+    weights_in(0, 2)
+    finish(3)
+    finish(2)
+    relay(7)
+    first(5)
+    direct(6)
+    weights_in(2, 5)
+    finish(1)
+    finish(0)
+    relay(6)
+    first(4)
+    direct(5)
+    weights_in(5, 8)
+    finish(7)
+    relay(5)
+    direct(4)
+    weights_in(8, 11)
+    finish(6)
+    relay(4)
+    weights_in(11, 14)
+    finish(5)
     weights_down(0, 14)
-    stores[2].start()
-    for k in (7, 6, 5, 4):
-        finish(k)
+    finish(4)
 
     for k in range(1, NZ):
         b_copy(k).wait_recv()
@@ -378,14 +406,12 @@
             for t in range(2):
                 z_copy(t, k).wait_send()
             b_copy(k).wait_send()
-    for store in stores:
-        store.wait()
-
-
-def experts_backward(tokens, cotangent, w_gate, w_up, w_down, pick, scale):
+
+
+def experts_backward(tokens, cotangent, w_gate, w_up, w_down, weight, count, slot):
     dim, hid = w_gate.shape
     bf, f32 = jnp.bfloat16, jnp.float32
-    vmem, hbm = pl.BlockSpec(memory_space=pltpu.VMEM), pl.BlockSpec(memory_space=pl.ANY)
+    vmem, hbm = pl.BlockSpec(memory_space=pltpu.VMEM), pl.BlockSpec(memory_space=pltpu.HBM)
     dma = pltpu.SemaphoreType.DMA
     message = pltpu.VMEM((8, 16, dim // Q), bf)
     side = dma((2, NZ))
@@ -398,8 +424,8 @@
             jax.ShapeDtypeStruct((dim, hid), bf),
             jax.ShapeDtypeStruct((hid, dim), bf),
         ),
-        in_specs=[hbm] * 5 + [vmem] * 2,
-        out_specs=(vmem, hbm, hbm, hbm),
+        in_specs=[hbm] * 5 + [vmem] * 3,
+        out_specs=(vmem,) * 4,
         scratch_shapes=[
             pltpu.VMEM((2,) + tokens.shape, bf),
             pltpu.VMEM((dim, 2 * hid), bf),
@@ -418,41 +444,23 @@
             pltpu.VMEM((2, NZ, 16, dim), bf),
             pltpu.VMEM((NZ, 16, dim), bf),
             message, message,
-            pltpu.VMEM((dim, hid), bf),
-            pltpu.VMEM((dim, hid), bf),
-            pltpu.VMEM((hid, dim), bf),
-            dma((5,)), dma((2,)), dma((3,)),
+            pltpu.VMEM((Q, 128, tokens.shape[0]), bf),
+            dma((5,)), dma((2,)),
             dma((2, 7)), dma((2, 7)), side, side,
             two_sides, two_sides, two_sides, two_sides,
             side, side, side, side, side, side,
             dma((NZ,)), dma((NZ,)), dma((7,)), dma((7,)),
         ],
         compiler_params=pltpu.CompilerParams(
-            collective_id=0, has_side_effects=True, vmem_limit_bytes=62 * 2**20
+            collective_id=0, has_side_effects=True, vmem_limit_bytes=45 * 2**20
         ),
         name="experts_backward",
-    )(tokens, cotangent, w_gate, w_up, w_down, pick, scale)
+    )(tokens, cotangent, w_gate, w_up, w_down, weight, count, slot)
 
 
 def body(tokens, cotangent, w_gate, w_up, w_down, gate_weight, counts, slots):
-    experts = counts.shape[1]
-    cap = slots.shape[2]
-    tok_dev = tokens.shape[0]
-    position = lax.broadcasted_iota(jnp.int32, (experts, cap), 1)
-    live = jnp.where(position < counts[0][:, None], gate_weight[0], jnp.zeros_like(gate_weight[0]))
-
-    def rows(a):
-        a = a.reshape(NX, 2, NC, cap).transpose(0, 2, 1, 3).reshape(experts * cap, 1)
-        return jnp.broadcast_to(a, (experts * cap, Q)).reshape(experts * cap * Q, 1)
-
-    slot_rows = rows(slots[0])
-    dims = (Q, experts * cap * Q, tok_dev)
-    pick = (
-        (slot_rows[None] == lax.broadcasted_iota(jnp.int32, dims, 2))
-        & (lax.broadcasted_iota(jnp.int32, dims, 1) % Q == lax.broadcasted_iota(jnp.int32, dims, 0))
-    ).astype(jnp.bfloat16)
     grad_tokens, grad_gate, grad_up, grad_down = experts_backward(
-        tokens, cotangent, w_gate[0], w_up[0], w_down[0], pick, rows(live)
+        tokens, cotangent, w_gate[0], w_up[0], w_down[0], gate_weight[0].T, counts, slots[0].T
     )
     return grad_tokens, grad_gate[None], grad_up[None], grad_down[None]
 

time: 255 us -> 230 us (0.902); the launches traced: 251 us -> 230 us
  Pallas kernels: 236 us -> 221 us
  local copies, waits for them, and re-layouts: 11.9 us -> 8.74 us
    pallas_call x1, Pallas kernels: 236 us -> 221 us  [experts_backward(): pl.pallas_call(kernel, out_shape=(jax.ShapeDtypeStruct(tokens.shape, bf),...]
    unnamed x9 -> x14, local copies, waits for them, and re-layouts: 8.88 us -> 8.74 us
where the time goes in v4:
time: 230 us
  Pallas kernels  221 us (96%)
  local copies, waits for them, and re-layouts  8.74 us (4%)
    pallas_call x1, Pallas kernels, experts_backward(): pl.pallas_call(kernel, out_shape=(jax.ShapeDtypeStruct(tokens.shape, bf),...  221 us
    unnamed x14, local copies, waits for them, and re-layouts  8.74 us

profile of v4, /device:TPU:1, one launch (start us, length us, event | category | flops | bytes accessed | tf_op | source)
XLA Modules:
  0.0 230.1 jit_solution(2185127766083075455)
XLA Ops:
  0.6 0.0 copy-start
  0.6 1.1 copy-done
  1.7 0.0 copy-start.1
  1.7 1.1 copy-done.1
  2.8 0.0 copy-start.2
  2.8 0.7 copy-done.2
  3.5 0.0 copy-start.3
  3.5 0.7 copy-done.3
  4.2 0.0 copy-start.4
  4.2 0.7 copy-done.4
  4.8 220.7 %experts_backward.1 = (bf16[48,7168]{1,0:T(8,128)(2,1)S(1)}, bf16[7168,128]{1,0:T(8,128)(2,1)S(1)}, bf16[7168,128]{1,0:T(8,128)(2,1)S(1)}, bf16[128,7168]{1,0:T(8,128)(2,1)S(1)}) custom-call(bf16[48,7168]{1,0:T(8,128)(2,1)S(1)} %copy-done, bf16[48,7168]{1,0:T(8,128)(2,1)S(1)} %copy-done.1, bf16[7168,128]{1,0:T(8,128)(2,1)} %bitcast.17, ...), custom_call_target="tpu_custom_call" | custom-call | tf_op jit(solution)/shard_map/experts_backward/pallas_call | solution.py:419
  225.5 0.8 copy.16
  226.4 1.2 copy.17
  227.6 1.2 copy.18
  228.8 1.2 copy.19
Async XLA Ops:
  0.6 1.1 copy-start
  1.7 1.1 copy-start.1
  2.8 0.7 copy-start.2
  3.5 0.7 copy-start.3
  4.2 0.7 copy-start.4
